TPU v7x, 256 devices: a whole 4x4x8 slice. The times are simulated.
256 devices in a mesh: gen: 8 (over z_lo, core), user: 16 (over x, y), cand: 2 (over z_hi).
Axes of the slice: x: 4, y: 4, z: 8 (z_hi: 2, z_lo: 4; z = z_hi * 4 + z_lo), core: 2. Of those that a mesh axis runs over, the one named last changes fastest.
Arguments:
- states: bfloat16 [16384, 4096], P(('user', 'cand')), may hold values from -6 to 6
- norm_gain: float32 [4096], replicated, may hold values from 0.1 to 1.9
- gate_weight: bfloat16 [4096, 7168], P('user', 'gen'), may hold values from -0.09375 to 0.09375
- up_weight: bfloat16 [4096, 7168], P('user', 'gen'), may hold values from -0.09375 to 0.09375
- down_weight: bfloat16 [7168, 4096], P('gen', 'user'), may hold values from -0.0625 to 0.0625
- proj_weight: bfloat16 [4096, 1024], P('gen'), may hold values from -0.09375 to 0.09375
- private_rows: bfloat16 [32768, 1024], P(('gen', 'user')), may hold values from -6 to 6
- enc_weight: bfloat16 [1024, 1024], replicated, may hold values from -0.1875 to 0.1875
- user_ids: int32 [32768], P(('gen', 'user')), may hold values from 0 to 31
Outputs:
- votes: float32 [16, 2, 128], P(None, 'cand')
Inputs may be any that keep to these rules, and one draw needn't show every extreme that they name: `user_ids`: a user is a pair of a block of 256 rows and a slot; no user has rows in two blocks.
All inputs are finite; a program needn't handle non-finite values.
Results may differ from a plain program's by a relative error of at most 0.0025.
Values may be sent and summed in bfloat16 or wider, within the bound.
No kernel may reach another device: no remote copies, remote signals or barrier semaphores. Data moves between devices by JAX's collectives and lax.ppermute only.
A program may use at most 128 MiB of HBM per device.

v0:
```python
import jax
import jax.numpy as jnp
from jax import lax
from jax.sharding import PartitionSpec as P

STEPS = 4
CAP = 8
USERS_DEV = 32


def unit_rows(matrix):
    return (matrix * lax.rsqrt(jnp.sum(matrix * matrix, axis=1, keepdims=True) + 1e-06)).astype(
        jnp.bfloat16
    )


def project_in(inputs, gate_part, up_part):

    def add_rows(piece):
        return jnp.dot(inputs, piece, preferred_element_type=jnp.float32)

    gate = add_rows(lax.all_gather(gate_part, "user", axis=0, tiled=True))
    up_proj = add_rows(lax.all_gather(up_part, "user", axis=0, tiled=True))
    return (gate, up_proj)


def shards(
    states,
    norm_gain,
    gate_weight,
    up_weight,
    down_weight,
    proj_weight,
    private_rows,
    enc_weight,
    user_ids,
):
    tok_rows, width_model = states.shape
    groups = tok_rows // STEPS
    values = states.astype(jnp.float32)
    normed = (
        values * lax.rsqrt(jnp.mean(values * values, axis=1, keepdims=True) + 1e-05) * norm_gain
    ).astype(jnp.bfloat16)
    gate_part, up_part, down_part = (gate_weight, up_weight, down_weight)
    gate, up_proj = project_in(normed, gate_part, up_part)
    hidden = (jax.nn.silu(gate) * up_proj).astype(jnp.bfloat16)
    mixed = jnp.dot(
        hidden,
        lax.all_gather(down_part, "user", axis=1, tiled=True),
        preferred_element_type=jnp.float32,
    )
    pooled_mlp = jnp.sum(mixed.reshape(-1, STEPS, width_model), axis=1)
    pooled_mlp = lax.psum_scatter(pooled_mlp, "gen", scatter_dimension=1, tiled=True)
    slab_width = pooled_mlp.shape[1]
    own_cols = lax.dynamic_slice_in_dim(values, lax.axis_index("gen") * slab_width, slab_width, 1)
    pooled_in = jnp.sum(own_cols.reshape(groups, STEPS, slab_width), axis=1)
    pooled = ((pooled_in + pooled_mlp) / STEPS).astype(jnp.bfloat16)
    partial_emb = jnp.dot(pooled, proj_weight, preferred_element_type=jnp.float32)
    embedding = lax.psum(partial_emb, "gen")
    candidate = unit_rows(embedding)
    every_cand = lax.all_gather(candidate, "user", axis=0, tiled=True)
    encoded = unit_rows(jnp.dot(private_rows, enc_weight, preferred_element_type=jnp.float32))
    scores = lax.dot_general(
        encoded, every_cand, (((1,), (1,)), ((), ())), preferred_element_type=jnp.float32
    )
    kernel = jnp.exp(scores * 60.0)
    totals = lax.psum(jnp.sum(kernel, axis=1), "cand")
    member = (user_ids[:, None] == jnp.arange(USERS_DEV, dtype=jnp.int32)[None, :]).astype(
        jnp.float32
    )
    counts = jnp.sum(member, axis=0)
    limit = jnp.minimum(1.0, CAP / jnp.maximum(counts, 1.0))
    row_cap = jnp.dot(member, limit, precision=lax.Precision.HIGHEST)
    row_total = private_rows.shape[0] * lax.axis_size("gen") * lax.axis_size("user")
    cand_total = every_cand.shape[0] * lax.axis_size("cand")
    weight_rows = row_cap / totals * (cand_total / row_total)
    partial_votes = jnp.dot(weight_rows, kernel, precision=lax.Precision.HIGHEST)
    votes = lax.psum(partial_votes, ("gen", "user"))
    return votes.reshape(lax.axis_size("user"), 1, groups)


def solution(mesh):
    return jax.shard_map(
        shards,
        mesh=mesh,
        in_specs=(
            P(("user", "cand"), None),
            P(),
            P("user", "gen"),
            P("user", "gen"),
            P("gen", "user"),
            P("gen", None),
            P(("gen", "user"), None),
            P(),
            P(("gen", "user")),
        ),
        out_specs=P(None, "cand", None),
        check_vma=False,
    )
```

profile of v0, /device:TPU:0, one launch (start us, length us, event | category | flops | bytes accessed | tf_op | source)
XLA Modules:
  0.0 810.1 jit_solution(10870717847516051505)
XLA Ops:
  6.5 0.0 copy-start
  6.5 0.0 copy-start.1
  6.5 0.0 all-gather.5.cloned.1.call-start
  6.5 0.7 all-gather.5.cloned.1.call-update
  7.3 0.0 all-gather.7.cloned.1.call-start
  7.3 0.7 all-gather.7.cloned.1.call-update
  8.0 0.0 all-gather.9.cloned.1.call-start
  8.1 0.7 all-gather.9.cloned.1.call-update
  8.7 0.0 reduce-scatter.2.cloned.1.call-start
  8.8 3.1 multiply_reduce_fusion
  11.9 70.3 %all-gather.5.cloned.1.call-done = bf16[4096,896]{1,0:T(8,128)(2,1)} async-done(((bf16[256,896]{1,0:T(8,128)(2,1)}), bf16[4096,896]{1,0:T(8,128)(2,1)}) %all-gather.5.cloned.1.call-update) | async-done | bytes 7340048 | tf_op jit(solution)/shard_map/all_gather | solution.py:22
  82.2 0.0 copy-done.1
  82.2 10.1 %fusion.1 = f32[512,896]{1,0:T(8,128)} fusion(bf16[4096,896]{1,0:T(8,128)(2,1)} %all-gather.5.cloned.1.call-done, f32[4096]{0:T(1024)S(1)} %copy-done.1, f32[512]{0:T(512)S(1)} %add_rsqrt_fusion, bf16[512,4096]{1,0:T(8,128)(2,1)} %param.9), kind=kOutput, calls=%fused_computation.5 | convolution fusion | flops 3766484992 | bytes 13387776 | tf_op jit(solution)/shard_map/dot_general | solution.py:20
  92.3 63.2 %all-gather.7.cloned.1.call-done = bf16[4096,896]{1,0:T(8,128)(2,1)} async-done(((bf16[256,896]{1,0:T(8,128)(2,1)}), bf16[4096,896]{1,0:T(8,128)(2,1)}) %all-gather.7.cloned.1.call-update) | async-done | bytes 7340048 | tf_op jit(solution)/shard_map/all_gather | solution.py:23
  155.6 79.3 %all-gather.9.cloned.1.call-done = bf16[896,4096]{1,0:T(8,128)(2,1)} async-done(((bf16[896,256]{1,0:T(8,128)(2,1)}), bf16[896,4096]{1,0:T(8,128)(2,1)}) %all-gather.9.cloned.1.call-update) | async-done | bytes 7340048 | tf_op jit(solution)/shard_map/all_gather | solution.py:49
  234.8 17.4 %fusion.2 = f32[512,4096]{1,0:T(8,128)} fusion(bf16[896,4096]{1,0:T(8,128)(2,1)} %all-gather.9.cloned.1.call-done, f32[512,896]{1,0:T(8,128)} %fusion.1, bf16[4096,896]{1,0:T(8,128)(2,1)} %all-gather.7.cloned.1.call-done, f32[4096]{0:T(1024)S(1)} %copy-done.1, f32[512]{0:T(512)S(1)} %add_rsqrt_fusion, bf16[512,4096]{1,0:T(8,128)(2,1)} %param.9), kind=kOutput, calls=%fused_computation.9 | convolution fusion | flops 7527333888 | bytes 29116416 | tf_op jit(solution)/shard_map/dot_general | solution.py:47
  252.2 9.8 %reshape.32 = f32[128,4,4096]{2,1,0:T(4,128)} reshape(f32[512,4096]{1,0:T(8,128)} %fusion.2) | data formatting | bytes 16777216 | tf_op jit(solution)/shard_map/reshape | solution.py:52
  262.0 10.0 %reduce_sum.67 = f32[128,4096]{1,0:T(8,128)} reduce(f32[128,4,4096]{2,1,0:T(4,128)} %reshape.32, f32[]{:T(128)} %constant.15.clone.1), dimensions={1}, to_apply=%region_4.5 | reduce | flops 1572864 | bytes 10485764 | tf_op jit(solution)/shard_map/reduce_sum | solution.py:52
  272.0 0.0 reduce-scatter.2.cloned.1.call-update
  272.1 0.0 all-reduce.2.cloned.1.call-start
  272.1 6.5 convert_element_type.23
  278.6 1.3 constant_dynamic-slice_fusion
  279.9 0.0 copy-start.2
  279.9 1.3 reshape.31
  281.2 1.8 reduce_sum.65
  283.1 29.9 %reduce-scatter.2.cloned.1.call-done = f32[128,512]{1,0:T(8,128)} async-done(((f32[128,4096]{1,0:T(8,128)}), f32[128,512]{1,0:T(8,128)}) %reduce-scatter.2.cloned.1.call-update) | async-done | bytes 262160 | tf_op jit(solution)/shard_map/reduce_scatter | solution.py:53
  313.0 2.4 fusion.4
  315.4 0.0 all-reduce.2.cloned.1.call-update
  315.4 0.3 all-gather.11.cloned.1.call-start
  315.7 70.7 %all-reduce.2.cloned.1.call-done = f32[128,1024]{1,0:T(8,128)} async-done(((f32[128,1024]{1,0:T(8,128)}), f32[128,1024]{1,0:T(8,128)}) %all-reduce.2.cloned.1.call-update) | async-done | bytes 524304 | tf_op jit(solution)/shard_map/psum | solution.py:59
  386.3 1.2 multiply_reduce_fusion.2
  387.5 1.8 multiply_convert_fusion.8
  389.3 0.0 all-gather.11.cloned.1.call-update
  389.4 0.0 copy-done.2
  389.4 0.1 convert_reduce_fusion
  389.5 0.0 copy-done
  389.5 1.8 multiply_reduce_fusion.1
  391.3 0.1 fusion.6
  391.5 53.5 %all-gather.11.cloned.1.call-done = bf16[2048,1024]{1,0:T(8,128)(2,1)} async-done(((bf16[128,1024]{1,0:T(8,128)(2,1)}), bf16[2048,1024]{1,0:T(8,128)(2,1)}) %all-gather.11.cloned.1.call-update) | async-done | bytes 4194320 | tf_op jit(solution)/shard_map/all_gather | solution.py:61
  445.0 4.9 fusion.16
  449.8 8.8 %psum.22 = f32[256]{0:T(256)S(1)} all-reduce(f32[256]{0:T(256)S(1)} %get-tuple-element.7), channel_id=1, replica_groups=mesh['gen'=8,'user'=16,'cand'=2] {'cand'}, use_global_device_ids=true, to_apply=%region_9.10 | all-reduce | flops 256 | bytes 2048 | tf_op jit(solution)/shard_map/psum | solution.py:67
  458.6 2.7 convolution_bitcast_fusion
  461.3 341.9 %psum.23 = f32[16,1,128]{2,1,0:T(1,128)} all-reduce(f32[16,1,128]{2,1,0:T(1,128)S(1)} %convolution_bitcast_fusion), channel_id=1, replica_groups=mesh['gen'=8,'user'=16,'cand'=2] {'gen','user'}, use_global_device_ids=true, to_apply=%region_10.11 | all-reduce | flops 2048 | bytes 16384 | tf_op jit(solution)/shard_map/psum | solution.py:78
  (4 shorter events, 0.0 us)
Async XLA Ops:
  6.5 383.0 %copy-start = (bf16[1024,1024]{1,0:T(8,128)(2,1)S(1)}, bf16[1024,1024]{1,0:T(8,128)(2,1)}, u32[]{:S(2)}) copy-start(bf16[1024,1024]{1,0:T(8,128)(2,1)} %param.16) | copy-start | bytes 6291460
  6.5 75.7 %copy-start.1 = (f32[4096]{0:T(1024)S(1)}, f32[4096]{0:T(1024)}, u32[]{:S(2)}) copy-start(f32[4096]{0:T(1024)} %param.10) | copy-start | bytes 49156
  6.5 75.7 %all-gather.5.cloned.1.call-start = ((), (), s32[]{:S(2)}) async-start(), calls=%async_computation.1 | async-start | bytes 7798784 | tf_op jit(solution)/shard_map/all_gather | solution.py:22
  7.3 148.3 %all-gather.7.cloned.1.call-start = ((), (), s32[]{:S(2)}) async-start(), calls=%async_computation.2 | async-start | bytes 7798784 | tf_op jit(solution)/shard_map/all_gather | solution.py:23
  8.0 226.8 %all-gather.9.cloned.1.call-start = ((), (), s32[]{:S(2)}) async-start(), calls=%async_computation.3 | async-start | bytes 7798784 | tf_op jit(solution)/shard_map/all_gather | solution.py:49
  8.7 304.2 %reduce-scatter.2.cloned.1.call-start = ((), (), s32[]{:S(2)}) async-start(), calls=%async_computation.4 | async-start | bytes 2359296 | tf_op jit(solution)/shard_map/reduce_scatter | solution.py:53
  272.1 114.3 %all-reduce.2.cloned.1.call-start = ((), (), s32[]{:S(2)}) async-start(), calls=%async_computation.5 | async-start | bytes 1048576 | tf_op jit(solution)/shard_map/psum | solution.py:59
  279.9 109.5 %copy-start.2 = (s32[256]{0:T(256)S(1)}, s32[256]{0:T(256)}, u32[]{:S(2)}) copy-start(s32[256]{0:T(256)} %param.17) | copy-start | bytes 3076
  315.4 129.5 %all-gather.11.cloned.1.call-start = ((), (), s32[]{:S(2)}) async-start(), calls=%async_computation.6 | async-start | bytes 4456448 | tf_op jit(solution)/shard_map/all_gather | solution.py:61
Sparse Core Ops, SparseCore 0:
  9.8 72.3 all-gather.4
  84.7 70.8 all-gather.6
  158.0 76.7 all-gather.8
  272.2 40.7 reduce-scatter.1
  315.5 70.7 all-reduce.1
  389.5 55.4 all-gather.10
where the time goes:
time: 811 us; the launch traced here: 810 us
  waiting for transfers between devices  369 us (45%)
  blocking collectives  351 us (43%)
  matrix products  39.5 us (5%)
  other arithmetic  24.6 us (3%)
  between operations  13.5 us (2%)
  local copies, waits for them, and re-layouts  12.4 us (2%)
    psum x1, blocking collectives, shards(): votes = lax.psum(partial_votes, ('gen', 'user'))  342 us
    all_gather x1, waiting for transfers between devices, shards(): lax.all_gather(down_part, 'user', axis=1, tiled=True)  79.3 us
    psum x1, waiting for transfers between devices, shards(): embedding = lax.psum(partial_emb, 'gen')  70.7 us
    all_gather x1, waiting for transfers between devices, project_in(): gate = add_rows(lax.all_gather(gate_part, 'user', axis=0, tiled=True))  70.3 us
    all_gather x1, waiting for transfers between devices, project_in(): up_proj = add_rows(lax.all_gather(up_part, 'user', axis=0, tiled=True))  63.2 us
    all_gather x1, waiting for transfers between devices, shards(): every_cand = lax.all_gather(candidate, 'user', axis=0, tiled=True)  53.5 us
    reduce_scatter x1, waiting for transfers between devices, shards(): lax.psum_scatter(pooled_mlp, 'gen', scatter_dimension=1, tiled=True)  29.9 us
    dot_general x1, matrix products, shards(): jnp.dot(hidden, lax.all_gather(down_part, 'user', axis=1, tiled=True), pr...  17.4 us
  transfers between devices with their start and end apart: 6, of which 6 were waited for; matrix products, arithmetic and copies ran while one was open for 3% of the time, Pallas kernels for 0%

commit v1 on v0

v1 whole, which is shorter than its diff:
```python
import jax
import jax.numpy as jnp
from jax import lax
from jax.experimental import pallas as pl
from jax.experimental.pallas import tpu as pltpu
from jax.sharding import Mesh, PartitionSpec as P

STEPS = 4
CAP = 8
USERS_DEV = 32
CHUNKS = 4
F32 = jnp.float32
BF16 = jnp.bfloat16


def z_index(z):
    return (z % 4) * 2 + z // 4


def shift_z(a, k):
    return lax.ppermute(a, ("zl", "zh"), [(z_index(z), z_index((z + k) % 8)) for z in range(8)])


def swap_core(a):
    return lax.ppermute(a, "core", [(0, 1), (1, 0)])


def shift(a, axis, k):
    return lax.ppermute(a, axis, [(i, (i + k) % 4) for i in range(4)])


def unit_rows(matrix):
    return (matrix * lax.rsqrt(jnp.sum(matrix * matrix, axis=1, keepdims=True) + 1e-06)).astype(BF16)


def pick(a, i, axis=0):
    return lax.dynamic_index_in_dim(a, i, axis, keepdims=False)


def half_weights(gate, up, down, c):
    def cut(w, axis):
        full = lax.dynamic_slice_in_dim(w, c * 512, 384, axis)
        rest = lax.dynamic_slice_in_dim(w, 384 + c * 64, 64, axis)
        return full, rest

    gf, gr = cut(gate, 1)
    uf, ur = cut(up, 1)
    df, dr = cut(down, 0)
    gu = jnp.concatenate([gf, uf, gr, ur], axis=1)
    dn = jnp.concatenate(
        [
            df[0:128],
            df[128:256],
            df[256:384],
            jnp.concatenate([dr[:, :128], dr[:, 128:]], axis=0),
        ],
        axis=1,
    )
    return jnp.concatenate([gu, dn], axis=0)


def relay_states(own, zl):
    up_got, dn_got = [], []
    for t in range(CHUNKS + 3):
        up = own[0, min(t, CHUNKS - 1)]
        dn = own[1, min(t, CHUNKS - 1)]
        if t > 0:
            up = jnp.where(zl == 3, up, up_got[-1])
            dn = jnp.where(zl == 0, dn, dn_got[-1])
        up_got.append(shift_z(up, 1))
        dn_got.append(shift_z(dn, -1))
    up = lax.dynamic_slice_in_dim(jnp.concatenate(up_got, 0), zl * own.shape[2], CHUNKS * own.shape[2], 0)
    dn = lax.dynamic_slice_in_dim(
        jnp.concatenate(dn_got, 0), (3 - zl) * own.shape[2], CHUNKS * own.shape[2], 0
    )
    return up, dn


def ring_z(a):
    h = a.shape[0] // 2
    left = shift_z(a, 1)
    right = shift_z(a, -1)
    far = jnp.concatenate([shift_z(left[:h], 1), shift_z(right[h:], -1)], 0)
    return jnp.stack([a, right, far, left], 0)


def ff_kernel(own_ref, ra_ref, rb_ref, w_ref, hp_ref, acc):
    k = pl.program_id(0)

    @pl.when(k == 0)
    def _():
        acc[...] = jnp.zeros_like(acc)

    w = jnp.concatenate([w_ref[i, 0:256, :] for i in range(4)], axis=0)
    acc[0:512, :] += jnp.dot(own_ref[...], w, preferred_element_type=F32)
    acc[512:768, :] += jnp.dot(ra_ref[...], w, preferred_element_type=F32)
    acc[768:1024, :] += jnp.dot(rb_ref[...], w, preferred_element_type=F32)

    @pl.when(k == 3)
    def _():
        row = lax.broadcasted_iota(jnp.int32, (64, 256), 0)
        col = lax.broadcasted_iota(jnp.int32, (64, 256), 1)
        pool = (col // STEPS == row).astype(BF16)
        lane = lax.broadcasted_iota(jnp.int32, (256, 128), 1)
        for i in range(4):
            rows = pl.ds(i * 256, 256)
            gate = acc[rows, 0:384]
            up = acc[rows, 384:768]
            last = acc[rows, 768:896]
            hidden = (jax.nn.silu(gate) * up).astype(BF16)
            rest = jnp.where(lane < 64, jax.nn.silu(last) * pltpu.roll(last, 64, 1), 0.0).astype(BF16)
            hp_ref[pl.ds(i * 64, 64), 0:384] = jnp.dot(pool, hidden, preferred_element_type=F32).astype(BF16)
            hp_ref[pl.ds(i * 64, 64), 384:512] = jnp.dot(pool, rest, preferred_element_type=F32).astype(BF16)


def feed_forward(own, ra, rb, weights):
    d = own.shape[1]
    return pl.pallas_call(
        ff_kernel,
        out_shape=jax.ShapeDtypeStruct((256, 512), BF16),
        grid=(4,),
        in_specs=[
            pl.BlockSpec((512, d // 4), lambda k: (0, k)),
            pl.BlockSpec((256, d // 4), lambda k: (0, k)),
            pl.BlockSpec((256, d // 4), lambda k: (0, k)),
            pl.BlockSpec((4, 384, 896), lambda k: (k, 0, 0)),
        ],
        out_specs=pl.BlockSpec((256, 512), lambda k: (0, 0)),
        scratch_shapes=[pltpu.VMEM((1024, 896), F32)],
        name="feed_forward",
    )(own, ra, rb, weights)


def w2_kernel(z_ref, d_ref, p_ref, out_ref, acc):
    k = pl.program_id(0)

    @pl.when(k == 0)
    def _():
        acc[...] = jnp.zeros_like(acc)

    for i in range(4):
        p = p_ref[i]
        for j in range(3):
            acc[pl.ds(j * 128, 128), :] += jnp.dot(
                d_ref[i, :, pl.ds(j * 256, 256)], p, preferred_element_type=F32
            )
        acc[384:448, :] += jnp.dot(d_ref[i, 0:64, 768:896], p[0:128], preferred_element_type=F32)
        acc[384:448, :] += jnp.dot(d_ref[i, 64:128, 768:896], p[128:256], preferred_element_type=F32)

    @pl.when(k == 3)
    def _():
        out_ref[...] = acc[...].astype(BF16)


def down_proj(weights, proj_cols, zl):
    return pl.pallas_call(
        w2_kernel,
        out_shape=jax.ShapeDtypeStruct((512, 256), BF16),
        grid_spec=pltpu.PrefetchScalarGridSpec(
            num_scalar_prefetch=1,
            grid=(4,),
            in_specs=[
                pl.BlockSpec((4, 128, 896), lambda k, z: (k, 2, 0)),
                pl.BlockSpec((pl.Squeezed(), 4, 256, 256), lambda k, z: (lax.rem(k - z[0] + 4, 4), 0, 0, 0)),
            ],
            out_specs=pl.BlockSpec((512, 256), lambda k, z: (0, 0)),
            scratch_shapes=[pltpu.VMEM((512, 256), F32)],
        ),
        name="down_proj",
    )(zl.reshape(1), weights, proj_cols)


def shards(states, norm_gain, gate, up, down, proj, rows, enc, ids):
    zl, core, c = lax.axis_index("zl"), lax.axis_index("core"), lax.axis_index("zh")
    y = lax.axis_index("y")
    gen = zl * 2 + core
    pack = half_weights(gate, up, down, c)
    weights = lax.all_gather(pack, ("x", "y"), axis=0)
    values = states.astype(F32)
    normed = (
        values * lax.rsqrt(jnp.mean(values * values, axis=1, keepdims=True) + 1e-05) * norm_gain
    ).astype(BF16)
    mine = pick(normed.reshape(2, 2, CHUNKS, -1, normed.shape[1]), core)
    got_up, got_dn = relay_states(mine, zl)
    part = jnp.concatenate([got_up, got_dn], 0)
    other = swap_core(part)
    encoded = unit_rows(jnp.dot(rows, enc, preferred_element_type=F32))
    cols = lax.dynamic_slice_in_dim(proj, y * 256, 256, 1)
    cols = jnp.concatenate([cols[i * 128 : (i + 1) * 128] for i in range(4)], axis=1)
    bundle = ring_z(jnp.concatenate([encoded, cols], 0))
    bundle2 = swap_core(bundle)
    both = jnp.stack([bundle, bundle2], 1)
    all_rows = both[:, :, :256]
    first = jnp.where(core == 0, bundle[:, 256:], bundle2[:, 256:])
    second = jnp.where(core == 0, bundle2[:, 256:], bundle[:, 256:])
    proj_cols = jnp.stack([first, second], 1)
    proj_cols = jnp.concatenate([proj_cols[..., i * 256 : (i + 1) * 256] for i in range(4)], axis=2)
    proj_cols = proj_cols.reshape(4, 4, 256, 256)
    pool = (jnp.arange(512)[None, :] // STEPS == jnp.arange(128)[:, None]).astype(BF16)
    state_cols = lax.dynamic_slice_in_dim(states, gen * 512, 512, 1)
    resid = jnp.dot(pool, state_cols, preferred_element_type=F32).astype(BF16)
    resid = jnp.dot(resid, proj, preferred_element_type=F32)
    w2_cols = down_proj(weights, proj_cols, zl)
    w2_parts = jnp.stack([w2_cols, shift(w2_cols, "y", -1), shift(w2_cols, "y", 2), shift(w2_cols, "y", 1)], 0)
    hp = feed_forward(normed, part, other, weights)
    hp_own, hp_a, hp_b = hp[:128], hp[128:192], hp[192:]
    hp_other = jnp.where(core == 0, jnp.concatenate([hp_a, hp_b], 0), jnp.concatenate([hp_b, hp_a], 0))
    hp_all = jnp.where(
        c == 0, jnp.concatenate([hp_own, hp_other], 0), jnp.concatenate([hp_other, hp_own], 0)
    )
    w2 = jnp.concatenate([pick(w2_parts, (i - y) % 4) for i in range(4)], axis=1)
    emb = jnp.dot(hp_all, w2, preferred_element_type=F32).reshape(2, 128, -1)
    emb = jnp.concatenate(
        [(emb[i] + jnp.where(c == i, resid, 0.0))[None] for i in range(2)], 0
    ) * (1.0 / STEPS)
    emb = emb.reshape(2, 4, 2, 16, -1)
    keep = pick(emb, core, 2)
    send = pick(emb, 1 - core, 2)
    emb = (keep + swap_core(send)).astype(BF16)
    emb = lax.all_to_all(emb.transpose(1, 0, 2, 3).reshape(8, 16, -1), ("zl", "zh"), 0, 0)
    candidate = unit_rows(jnp.sum(emb.astype(F32), axis=0))
    cands = lax.all_to_all(
        jnp.broadcast_to(candidate[None], (16,) + candidate.shape), ("x", "y"), 0, 0
    ).reshape(256, -1)
    scores = lax.dot_general(
        cands, all_rows.reshape(2048, -1), (((1,), (1,)), ((), ())), preferred_element_type=F32
    )
    kernel = jnp.exp(scores * 60.0)
    totals = jnp.sum(kernel, axis=0).reshape(4, 2, 256)
    totals = jnp.roll(jnp.roll(totals, zl, 0), core, 1)
    member = (ids[:, None] == jnp.arange(USERS_DEV, dtype=jnp.int32)[None, :]).astype(F32)
    counts = jnp.sum(member, axis=0)
    limit = jnp.minimum(1.0, CAP / jnp.maximum(counts, 1.0))
    row_cap = jnp.dot(member, limit, precision=lax.Precision.HIGHEST)
    note = jnp.concatenate([totals.reshape(16, 128), row_cap.reshape(2, 128)], 0)
    notes = lax.all_to_all(jnp.broadcast_to(note[None], (16, 18, 128)), ("zl", "core", "zh"), 0, 0)
    totals = jnp.sum(notes[:, :16], axis=0).reshape(4, 2, 256)
    caps = notes[:, 16:].reshape(4, 2, 2, 256)[:, :, 0]
    weight = caps / totals * (4096 / 32768)
    weight = jnp.roll(jnp.roll(weight, -zl, 0), -core, 1)
    partial = jnp.sum(kernel * weight.reshape(1, 2048), axis=1)
    partial = lax.all_to_all(
        jnp.broadcast_to(partial.reshape(1, 2, 128), (128, 2, 128)), ("zl", "core", "x", "y"), 0, 0
    )
    votes = jnp.sum(partial.reshape(8, 16, 16, 16), axis=1)
    return votes.transpose(1, 0, 2).reshape(16, 1, 128)


def solution(mesh):
    fine = Mesh(mesh.devices.reshape(4, 2, 4, 4, 2), ("zl", "core", "x", "y", "zh"))
    gen, user, cand = ("zl", "core"), ("x", "y"), "zh"
    return jax.shard_map(
        shards,
        mesh=fine,
        in_specs=(
            P(user + (cand,), None),
            P(),
            P(user, gen),
            P(user, gen),
            P(gen, user),
            P(gen, None),
            P(gen + user, None),
            P(),
            P(gen + user),
        ),
        out_specs=P(None, cand, None),
        check_vma=False,
    )
```

time: 811 us -> 243 us (0.30)
  blocking collectives: 351 us -> 29.9 us
  waiting for transfers between devices: 369 us -> 72 us
  starting transfers between devices: 0.42 us -> 43.9 us
  matrix products: 39.5 us -> 8.69 us
  Pallas kernels: 0 us -> 18.4 us
  local copies, waits for them, and re-layouts: 12.4 us -> 20.7 us
    psum x2 -> x0, blocking collectives: 351 us -> none  [the longest x1 342 us: shards(): votes = lax.psum(partial_votes, ('gen', 'user'))]
    all_gather x4 -> x1, waiting for transfers between devices: 266 us -> 0.01 us  [shards(): weights = lax.all_gather(pack, ('x', 'y'), axis=0)]
    psum x1 -> x0, waiting for transfers between devices: 70.7 us -> none  [shards(): embedding = lax.psum(partial_emb, 'gen')]
    ppermute x0 -> x24, waiting for transfers between devices: none -> 56.4 us  [the longest x18 54.5 us: shift_z(): lax.ppermute(a, ('zl', 'zh'), [(z_index(z), z_index((z + k) % 8)) for z i...]
    ppermute x0 -> x24, starting transfers between devices: none -> 31.6 us  [the longest x18 27 us: shift_z(): lax.ppermute(a, ('zl', 'zh'), [(z_index(z), z_index((z + k) % 8)) for z i...]
    dot_general x6 -> x4, matrix products: 39.3 us -> 8.57 us  [the longest x1 4.9 us: shards(): lax.dot_general(cands, all_rows.reshape(2048, -1), (((1,), (1,)), ((), ()...]
    reduce_scatter x1 -> x0, waiting for transfers between devices: 29.9 us -> none  [shards(): lax.psum_scatter(pooled_mlp, 'gen', scatter_dimension=1, tiled=True)]
    all_to_all x0 -> x2, blocking collectives: none -> 29.9 us  [the longest x1 15.7 us: shards(): lax.all_to_all(jnp.broadcast_to(partial.reshape(1, 2, 128), (128, 2, 128)...]
  transfers between devices with their start and end apart: 6 -> 27, of which waited for: 6 -> 14; matrix products, arithmetic and copies ran while one was open for 3% -> 16% of each run, Pallas kernels for 0% -> 8%
where the time goes in v1:
time: 243 us; the launch traced here: 239 us
  waiting for transfers between devices  72 us (30%)
  starting transfers between devices  43.9 us (18%)
  other arithmetic  31.8 us (13%)
  blocking collectives  29.9 us (12%)
  local copies, waits for them, and re-layouts  20.7 us (9%)
  Pallas kernels  18.4 us (8%)
  between operations  14 us (6%)
  matrix products  8.69 us (4%)
    ppermute x18, waiting for transfers between devices, shift_z(): lax.ppermute(a, ('zl', 'zh'), [(z_index(z), z_index((z + k) % 8)) for z i...  54.5 us
    ppermute x18, starting transfers between devices, shift_z(): lax.ppermute(a, ('zl', 'zh'), [(z_index(z), z_index((z + k) % 8)) for z i...  27 us
    all_to_all x1, blocking collectives, shards(): lax.all_to_all(jnp.broadcast_to(partial.reshape(1, 2, 128), (128, 2, 128)...  15.7 us
    all_to_all x1, blocking collectives, shards(): lax.all_to_all(emb.transpose(1, 0, 2, 3).reshape(8, 16, -1), ('zl', 'zh')...  14.2 us
    pallas_call x1, Pallas kernels, feed_forward(): pl.pallas_call(ff_kernel, out_shape=jax.ShapeDtypeStruct((256, 512), BF16...  13.4 us
    all_to_all x1, waiting for transfers between devices, shards(): lax.all_to_all(jnp.broadcast_to(note[None], (16, 18, 128)), ('zl', 'core'...  10.9 us
    select_n x6, other arithmetic, relay_states(): up = jnp.where(zl == 3, up, up_got[-1])  10.6 us
    another operation x2, other arithmetic, shards(): both = jnp.stack([bundle, bundle2], 1)  6.54 us
  transfers between devices with their start and end apart: 27, of which 14 were waited for; matrix products, arithmetic and copies ran while one was open for 16% of the time, Pallas kernels for 8%

profile of v1, /device:TPU:0, one launch (start us, length us, event | category | flops | bytes accessed | tf_op | source)
XLA Modules:
  0.0 239.4 jit_solution(16418530750413033179)
XLA Ops:
  6.5 1.2 constant_dynamic-slice_fusion.9
  7.8 1.0 constant_dynamic-slice_fusion.7
  8.7 0.7 constant_dynamic-slice_fusion.1
  9.5 0.9 constant_dynamic-slice_fusion.3
  10.4 1.0 maximum_maximum_fusion.1
  11.5 3.2 %fusion = f32[512]{0:T(512)S(1)} fusion(bf16[512,4096]{1,0:T(8,128)(2,1)} %param.13), kind=kLoop, calls=%fused_computation.2 | loop fusion | flops 6290944 | bytes 4196352 | tf_op jit(solution)/shard_map/reduce_sum | solution.py:181
  14.9 1.7 fusion.2.own_ref
  16.8 1.8 copy-done.2
  18.6 1.3 copy-done.4
  20.1 10.2 %collective-permute-done = bf16[32,4096]{1,0:T(8,128)(2,1)S(1)} collective-permute-done((bf16[32,4096]{1,0:T(8,128)(2,1)S(1)}, bf16[32,4096]{1,0:T(8,128)(2,1)S(1)}, u32[]{:S(2)}, u32[]{:S(2)}) %collective-permute-start) | collective-permute-done | bytes 262176 | tf_op jit(solution)/shard_map/ppermute | solution.py:21
  30.3 1.7 fusion.23
  32.1 3.2 %collective-permute-start.7 = (bf16[32,4096]{1,0:T(8,128)(2,1)S(1)}, bf16[32,4096]{1,0:T(8,128)(2,1)S(1)}, u32[]{:S(2)}, u32[]{:S(2)}) collective-permute-start(bf16[32,4096]{1,0:T(8,128)(2,1)S(1)} %get-tuple-element.20), channel_id=1, source_target_pairs={{0,193},{64,0},{128,64},{192,128},{1,192},{65,1},{129,65},{193,129... | collective-permute-start | bytes 786440 | tf_op jit(solution)/shard_map/ppermute | solution.py:21
  35.3 5.4 %collective-permute-done.1 = bf16[32,4096]{1,0:T(8,128)(2,1)S(1)} collective-permute-done((bf16[32,4096]{1,0:T(8,128)(2,1)S(1)}, bf16[32,4096]{1,0:T(8,128)(2,1)S(1)}, u32[]{:S(2)}, u32[]{:S(2)}) %collective-permute-start.1) | collective-permute-done | bytes 262176 | tf_op jit(solution)/shard_map/ppermute | solution.py:21
  40.8 1.7 fusion.22
  42.5 1.7 multiply_reduce_fusion.1
  44.2 6.3 %collective-permute-done.2 = bf16[32,4096]{1,0:T(8,128)(2,1)} collective-permute-done((bf16[32,4096]{1,0:T(8,128)(2,1)S(1)}, bf16[32,4096]{1,0:T(8,128)(2,1)}, u32[]{:S(2)}, u32[]{:S(2)}) %collective-permute-start.2) | collective-permute-done | bytes 262176 | tf_op jit(solution)/shard_map/ppermute | solution.py:21
  50.5 2.2 broadcast_select_fusion.7
  52.7 3.2 %collective-permute-start.8 = (bf16[32,4096]{1,0:T(8,128)(2,1)}, bf16[32,4096]{1,0:T(8,128)(2,1)}, u32[]{:S(2)}, u32[]{:S(2)}) collective-permute-start(bf16[32,4096]{1,0:T(8,128)(2,1)} %get-tuple-element.18), channel_id=1, source_target_pairs={{0,193},{64,0},{128,64},{192,128},{1,192},{65,1},{129,65},{193,129... | collective-permute-start | bytes 786440 | tf_op jit(solution)/shard_map/ppermute | solution.py:21
  56.1 1.0 constant_dynamic-slice_fusion
  57.7 1.0 maximum_maximum_fusion
  58.7 3.2 %collective-permute-start.15 = (bf16[384,1024]{1,0:T(8,128)(2,1)}, bf16[384,1024]{1,0:T(8,128)(2,1)}, u32[]{:S(2)}, u32[]{:S(2)}) collective-permute-start(bf16[384,1024]{1,0:T(8,128)(2,1)} %maximum_maximum_fusion), channel_id=1, source_target_pairs={{0,193},{64,0},{128,64},{192,128},{1,192},{65,1},{129,65},{193,129... | collective-permute-start | bytes 2359304 | tf_op jit(solution)/shard_map/ppermute | solution.py:21
  61.9 2.1 broadcast_select_fusion.6
  64.0 3.2 %collective-permute-start.9 = (bf16[32,4096]{1,0:T(8,128)(2,1)}, bf16[32,4096]{1,0:T(8,128)(2,1)}, u32[]{:S(2)}, u32[]{:S(2)}) collective-permute-start(bf16[32,4096]{1,0:T(8,128)(2,1)} %get-tuple-element.16), channel_id=1, source_target_pairs={{0,193},{64,0},{128,64},{192,128},{1,192},{65,1},{129,65},{193,129... | collective-permute-start | bytes 786440 | tf_op jit(solution)/shard_map/ppermute | solution.py:21
  67.3 13.2 %collective-permute-done.16 = bf16[384,1024]{1,0:T(8,128)(2,1)S(1)} collective-permute-done((bf16[384,1024]{1,0:T(8,128)(2,1)}, bf16[384,1024]{1,0:T(8,128)(2,1)S(1)}, u32[]{:S(2)}, u32[]{:S(2)}) %collective-permute-start.16) | collective-permute-done | bytes 786464 | tf_op jit(solution)/shard_map/ppermute | solution.py:21
  80.8 1.0 slice.159
  81.8 3.3 %collective-permute-start.18 = (bf16[192,1024]{1,0:T(8,128)(2,1)S(1)}, bf16[192,1024]{1,0:T(8,128)(2,1)S(1)}, u32[]{:S(2)}, u32[]{:S(2)}) collective-permute-start(bf16[192,1024]{1,0:T(8,128)(2,1)S(1)} %slice.159), channel_id=1, source_target_pairs={{0,193},{64,0},{128,64},{192,128},{1,192},{65,1},{129,65},{193,129... | collective-permute-start | bytes 1179656 | tf_op jit(solution)/shard_map/ppermute | solution.py:21
  85.1 1.1 collective-permute-done.4
  86.2 2.0 broadcast_select_fusion.5
  88.2 3.2 %collective-permute-start.10 = (bf16[32,4096]{1,0:T(8,128)(2,1)S(1)}, bf16[32,4096]{1,0:T(8,128)(2,1)S(1)}, u32[]{:S(2)}, u32[]{:S(2)}) collective-permute-start(bf16[32,4096]{1,0:T(8,128)(2,1)S(1)} %get-tuple-element.14), channel_id=1, source_target_pairs={{0,193},{64,0},{128,64},{192,128},{1,192},{65,1},{129,65},{193,129... | collective-permute-start | bytes 786440 | tf_op jit(solution)/shard_map/ppermute | solution.py:21
  91.5 2.5 %collective-permute-done.17 = bf16[192,1024]{1,0:T(8,128)(2,1)S(1)} collective-permute-done((bf16[192,1024]{1,0:T(8,128)(2,1)S(1)}, bf16[192,1024]{1,0:T(8,128)(2,1)S(1)}, u32[]{:S(2)}, u32[]{:S(2)}) %collective-permute-start.17) | collective-permute-done | bytes 393248 | tf_op jit(solution)/shard_map/ppermute | solution.py:21
  94.1 2.5 %collective-permute-done.10 = bf16[32,4096]{1,0:T(8,128)(2,1)S(1)} collective-permute-done((bf16[32,4096]{1,0:T(8,128)(2,1)S(1)}, bf16[32,4096]{1,0:T(8,128)(2,1)S(1)}, u32[]{:S(2)}, u32[]{:S(2)}) %collective-permute-start.10) | collective-permute-done | bytes 262176 | tf_op jit(solution)/shard_map/ppermute | solution.py:21
  96.6 2.4 %collective-permute-done.5 = bf16[32,4096]{1,0:T(8,128)(2,1)S(1)} collective-permute-done((bf16[32,4096]{1,0:T(8,128)(2,1)S(1)}, bf16[32,4096]{1,0:T(8,128)(2,1)S(1)}, u32[]{:S(2)}, u32[]{:S(2)}) %collective-permute-start.5) | collective-permute-done | bytes 262176 | tf_op jit(solution)/shard_map/ppermute | solution.py:21
  99.0 0.8 broadcast_select_fusion.4
  99.8 1.3 collective-permute-start.11
  101.1 3.9 %fusion.53 = (bf16[4,1,384,1024]{3,2,0,1:T(8,128)(2,1)}, bf16[4,384,1024]{2,1,0:T(8,128)(2,1)}) fusion(bf16[1,384,1024]{2,1,0:T(8,128)(2,1)S(1)} %bitcast.115, bf16[1,384,1024]{2,1,0:T(8,128)(2,1)S(1)} %maximum_bitcast_fusion, bf16[1,384,1024]{2,1,0:T(8,128)(2,1)} %bitcast.13, bf16[1,384,1024]{2,1,0:T(8,128)(2,1)S(1)} %fusion.64), kind=kLoop, calls=%fused_computation.153 | loop fusion | flops 4718592 | bytes 9437184 | tf_op jit(solution)/shard_map/stack | solution.py:192
  105.0 0.8 collective-permute-start.6
  106.3 2.5 %collective-permute-start.12 = (bf16[32,4096]{1,0:T(8,128)(2,1)S(1)}, bf16[32,4096]{1,0:T(8,128)(2,1)S(1)}, u32[]{:S(2)}, u32[]{:S(2)}) collective-permute-start(bf16[32,4096]{1,0:T(8,128)(2,1)S(1)} %get-tuple-element.59), channel_id=1, source_target_pairs={{0,193},{64,0},{128,64},{192,128},{1,192},{65,1},{129,65},{193,129... | collective-permute-start | bytes 786440 | tf_op jit(solution)/shard_map/ppermute | solution.py:21
  108.8 6.1 %collective-permute-done.6 = bf16[32,4096]{1,0:T(8,128)(2,1)S(1)} collective-permute-done((bf16[32,4096]{1,0:T(8,128)(2,1)S(1)}, bf16[32,4096]{1,0:T(8,128)(2,1)S(1)}, u32[]{:S(2)}, u32[]{:S(2)}) %collective-permute-start.6) | collective-permute-done | bytes 262176 | tf_op jit(solution)/shard_map/ppermute | solution.py:21
  115.7 2.5 %collective-permute-start.13 = (bf16[32,4096]{1,0:T(8,128)(2,1)S(1)}, bf16[32,4096]{1,0:T(8,128)(2,1)S(1)}, u32[]{:S(2)}, u32[]{:S(2)}) collective-permute-start(bf16[32,4096]{1,0:T(8,128)(2,1)S(1)} %get-tuple-element.57), channel_id=1, source_target_pairs={{0,193},{64,0},{128,64},{192,128},{1,192},{65,1},{129,65},{193,129... | collective-permute-start | bytes 786440 | tf_op jit(solution)/shard_map/ppermute | solution.py:21
  118.1 1.3 constant_dynamic-slice_fusion.12
  119.5 4.2 %collective-permute-done.13 = bf16[32,4096]{1,0:T(8,128)(2,1)S(1)} collective-permute-done((bf16[32,4096]{1,0:T(8,128)(2,1)S(1)}, bf16[32,4096]{1,0:T(8,128)(2,1)S(1)}, u32[]{:S(2)}, u32[]{:S(2)}) %collective-permute-start.13) | collective-permute-done | bytes 262176 | tf_op jit(solution)/shard_map/ppermute | solution.py:21
  123.7 1.6 pad_maximum_fusion.3.ra_ref
  125.3 1.7 select_bitcast_fusion.1
  127.4 1.5 copy.20
  128.9 5.0 %down_proj.1 = bf16[512,256]{1,0:T(8,128)(2,1)} custom-call(s32[1]{0:T(128)} %bitcast.11.z_ref, bf16[16,384,896]{2,1,0:T(8,128)(2,1)} %bitcast.108, bf16[4,4,256,256]{3,2,1,0:T(8,128)(2,1)} %bitcast.111), custom_call_target="tpu_custom_call" | custom-call | tf_op jit(solution)/shard_map/down_proj/pallas_call | solution.py:156
  133.9 3.2 %collective-permute-start.20 = (bf16[512,256]{1,0:T(8,128)(2,1)}, bf16[512,256]{1,0:T(8,128)(2,1)S(1)}, u32[]{:S(2)}, u32[]{:S(2)}) collective-permute-start(bf16[512,256]{1,0:T(8,128)(2,1)} %down_proj.1), channel_id=1, source_target_pairs={{0,6},{2,0},{4,2},{6,4},{1,7},{3,1},{5,3},{7,5},{8,14},{10,8},{12,... | collective-permute-start | bytes 786440 | tf_op jit(solution)/shard_map/ppermute | solution.py:29
  137.5 1.0 collective-permute-start.22
  138.5 13.4 %feed_forward.1 = bf16[256,512]{1,0:T(8,128)(2,1)} custom-call(bf16[512,4096]{1,0:T(8,128)(2,1)} %copy-done.2, bf16[256,4096]{1,0:T(8,128)(2,1)} %pad_maximum_fusion.3.ra_ref, bf16[256,4096]{1,0:T(8,128)(2,1)} %collective-permute-done.14.rb_ref, bf16[16,384,896]{2,1,0:T(8,128)(2,1)} %bitcast.109), custom_call_target="tpu_custom_call" | custom-call | tf_op jit(solution)/shard_map/feed_forward/pallas_call | solution.py:118
  151.9 0.9 fusion.55
  152.8 1.0 fusion.54
  154.5 0.8 copy-done.7
  155.3 1.5 slice_add_fusion.1
  157.2 1.9 collective-permute-done.23
  159.2 14.2 %all_to_all.20 = bf16[8,16,1024]{2,1,0:T(8,128)(2,1)S(1)} all-to-all(bf16[8,16,1024]{2,1,0:T(8,128)(2,1)S(1)} %bitcast.116), channel_id=1, replica_groups=mesh['zl'=4,'core'=2,'x'=4,'y'=4,'zh'=2] {'zl','zh'}, dimensions={0} | all-to-all | bytes 524288 | tf_op jit(solution)/shard_map/all_to_all | solution.py:220
  173.6 0.9 broadcast_in_dim.14
  174.4 6.0 %all-to-all-start.1 = ((bf16[16,16,1024]{2,1,0:T(8,128)(2,1)}), bf16[16,16,1024]{2,1,0:T(8,128)(2,1)S(1)}, u32[]{:S(2)}, u32[]{:S(2)}) async-start(bf16[16,16,1024]{2,1,0:T(8,128)(2,1)} %broadcast_in_dim.14), calls=%async_computation.1 | async-start | bytes 1048576 | tf_op jit(solution)/shard_map/all_to_all | solution.py:222
  180.8 2.7 %pad_maximum_fusion = bf16[4,2,256,1024]{3,2,0,1:T(8,128)(2,1)S(1)} fusion(bf16[4,1,384,1024]{3,2,0,1:T(8,128)(2,1)} %bitcast.35, bf16[4,1,384,1024]{3,2,0,1:T(8,128)(2,1)} %get-tuple-element.9), kind=kLoop, calls=%fused_computation.5 | loop fusion | flops 8388608 | bytes 10485760 | tf_op jit(solution)/shard_map/stack | solution.py:192
  183.4 2.4 %copy.23 = bf16[4,2,256,1024]{3,2,1,0:T(8,128)(2,1)} copy(bf16[4,2,256,1024]{3,2,0,1:T(8,128)(2,1)S(1)} %pad_maximum_fusion) | data formatting | bytes 8388608 | tf_op jit(solution)/shard_map/slice | solution.py:193
  185.8 4.7 %all-to-all-done.1 = bf16[16,16,1024]{2,1,0:T(8,128)(2,1)S(1)} async-done(((bf16[16,16,1024]{2,1,0:T(8,128)(2,1)}), bf16[16,16,1024]{2,1,0:T(8,128)(2,1)S(1)}, u32[]{:S(2)}, u32[]{:S(2)}) %all-to-all-start.1) | async-done | bytes 524320 | tf_op jit(solution)/shard_map/all_to_all | solution.py:222
  190.6 4.9 %fusion.58 = (f32[2048]{0:T(1024)S(1)}, f32[256,2048]{1,0:T(8,128)}) fusion(bf16[256,1024]{1,0:T(8,128)(2,1)S(1)} %bitcast.118, bf16[2048,1024]{1,0:T(8,128)(2,1)} %bitcast.112), kind=kOutput, calls=%fused_computation.156 | convolution fusion | flops 1074788352 | bytes 6823936 | tf_op jit(solution)/shard_map/dot_general | solution.py:225
  196.3 6.2 %all-to-all-start.2 = ((f32[16,18,128]{2,1,0:T(8,128)}), f32[16,18,128]{2,1,0:T(8,128)S(1)}, u32[]{:S(2)}, u32[]{:S(2)}) async-start(f32[16,18,128]{2,1,0:T(8,128)} %broadcast_in_dim.15), calls=%async_computation.2 | async-start | bytes 393216 | tf_op jit(solution)/shard_map/all_to_all | solution.py:236
  202.5 10.9 %all-to-all-done.2 = f32[16,18,128]{2,1,0:T(8,128)S(1)} async-done(((f32[16,18,128]{2,1,0:T(8,128)}), f32[16,18,128]{2,1,0:T(8,128)S(1)}, u32[]{:S(2)}, u32[]{:S(2)}) %all-to-all-start.2) | async-done | bytes 147488 | tf_op jit(solution)/shard_map/all_to_all | solution.py:236
  213.6 2.0 multiply_reduce_fusion
  215.6 15.7 %all_to_all.21 = f32[128,2,128]{2,1,0:T(2,128)S(1)} all-to-all(f32[128,2,128]{2,1,0:T(2,128)S(1)} %broadcast_in_dim.17), channel_id=1, replica_groups=mesh['zl'=4,'core'=2,'x'=4,'y'=4,'zh'=2] {'zl','core','x','y'}, dimensions={0} | all-to-all | bytes 262144 | tf_op jit(solution)/shard_map/all_to_all | solution.py:242
  (108 shorter events, 7.8 us)
Async XLA Ops:
  6.5 36.0 %copy-start = (bf16[1024,1024]{1,0:T(8,128)(2,1)S(1)}, bf16[1024,1024]{1,0:T(8,128)(2,1)}, u32[]{:S(2)}) copy-start(bf16[1024,1024]{1,0:T(8,128)(2,1)} %param.20) | copy-start | bytes 6291460
  6.5 122.3 %all-gather.3.cloned.1.call-start = ((), (), s32[]{:S(2)}) async-start(), calls=%async_computation.4 | async-start | bytes 11698176 | tf_op jit(solution)/shard_map/all_gather | solution.py:178
  11.4 3.3 %copy-start.15 = (f32[4096]{0:T(1024)S(1)}, f32[4096]{0:T(1024)}, u32[]{:S(2)}) copy-start(f32[4096]{0:T(1024)} %param.14) | copy-start | bytes 49156
  11.5 3.5 %copy-start.3 = (bf16[512,4096]{1,0:T(8,128)(2,1)S(1)}, bf16[512,4096]{1,0:T(8,128)(2,1)}, u32[]{:S(2)}) copy-start(bf16[512,4096]{1,0:T(8,128)(2,1)} %param.13) | copy-start | bytes 12582916
  16.6 2.0 copy-start.2
  18.6 1.3 copy-start.4
  18.6 23.9 %copy-start.14 = (bf16[256,1024]{1,0:T(8,128)(2,1)S(1)}, bf16[256,1024]{1,0:T(8,128)(2,1)}, u32[]{:S(2)}) copy-start(bf16[256,1024]{1,0:T(8,128)(2,1)} %param.19) | copy-start | bytes 1572868
  19.9 10.5 %collective-permute-start = (bf16[32,4096]{1,0:T(8,128)(2,1)S(1)}, bf16[32,4096]{1,0:T(8,128)(2,1)S(1)}, u32[]{:S(2)}, u32[]{:S(2)}) collective-permute-start(bf16[32,4096]{1,0:T(8,128)(2,1)S(1)} %get-tuple-element.19), channel_id=1, source_target_pairs={{0,64},{64,128},{128,192},{192,1},{1,65},{65,129},{129,193},{193,0... | collective-permute-start | bytes 786440 | tf_op jit(solution)/shard_map/ppermute | solution.py:21
  32.1 8.7 %collective-permute-start.1 = (bf16[32,4096]{1,0:T(8,128)(2,1)S(1)}, bf16[32,4096]{1,0:T(8,128)(2,1)S(1)}, u32[]{:S(2)}, u32[]{:S(2)}) collective-permute-start(bf16[32,4096]{1,0:T(8,128)(2,1)S(1)} %get-tuple-element.55), channel_id=1, source_target_pairs={{0,64},{64,128},{128,192},{192,1},{1,65},{65,129},{129,193},{193,0... | collective-permute-start | bytes 786440 | tf_op jit(solution)/shard_map/ppermute | solution.py:21
  32.1 12.1 %collective-permute-start.7 = (bf16[32,4096]{1,0:T(8,128)(2,1)S(1)}, bf16[32,4096]{1,0:T(8,128)(2,1)S(1)}, u32[]{:S(2)}, u32[]{:S(2)}) collective-permute-start(bf16[32,4096]{1,0:T(8,128)(2,1)S(1)} %get-tuple-element.20), channel_id=1, source_target_pairs={{0,193},{64,0},{128,64},{192,128},{1,192},{65,1},{129,65},{193,129... | collective-permute-start | bytes 786440 | tf_op jit(solution)/shard_map/ppermute | solution.py:21
  42.5 8.0 %collective-permute-start.2 = (bf16[32,4096]{1,0:T(8,128)(2,1)S(1)}, bf16[32,4096]{1,0:T(8,128)(2,1)}, u32[]{:S(2)}, u32[]{:S(2)}) collective-permute-start(bf16[32,4096]{1,0:T(8,128)(2,1)S(1)} %get-tuple-element.53), channel_id=1, source_target_pairs={{0,64},{64,128},{128,192},{192,1},{1,65},{65,129},{129,193},{193,0... | collective-permute-start | bytes 786440 | tf_op jit(solution)/shard_map/ppermute | solution.py:21
  44.2 11.7 %copy-start.6 = (f32[256,1024]{1,0:T(8,128)S(1)}, f32[256,1024]{1,0:T(8,128)}, u32[]{:S(2)}) copy-start(f32[256,1024]{1,0:T(8,128)} %get-tuple-element.62) | copy-start | bytes 3145732
  52.7 9.2 %copy-start.5 = (bf16[2,4,32,4096]{3,2,1,0:T(8,128)(2,1)S(1)}, bf16[2,4,32,4096]{3,2,1,0:T(8,128)(2,1)}, u32[]{:S(2)}) copy-start(bf16[2,4,32,4096]{3,2,1,0:T(8,128)(2,1)} %copy-done.4) | copy-start | bytes 6291460
  52.7 9.2 %collective-permute-start.3 = (bf16[32,4096]{1,0:T(8,128)(2,1)}, bf16[32,4096]{1,0:T(8,128)(2,1)}, u32[]{:S(2)}, u32[]{:S(2)}) collective-permute-start(bf16[32,4096]{1,0:T(8,128)(2,1)} %get-tuple-element.17), channel_id=1, source_target_pairs={{0,64},{64,128},{128,192},{192,1},{1,65},{65,129},{129,193},{193,0... | collective-permute-start | bytes 786440 | tf_op jit(solution)/shard_map/ppermute | solution.py:21
  52.7 9.2 %collective-permute-start.8 = (bf16[32,4096]{1,0:T(8,128)(2,1)}, bf16[32,4096]{1,0:T(8,128)(2,1)}, u32[]{:S(2)}, u32[]{:S(2)}) collective-permute-start(bf16[32,4096]{1,0:T(8,128)(2,1)} %get-tuple-element.18), channel_id=1, source_target_pairs={{0,193},{64,0},{128,64},{192,128},{1,192},{65,1},{129,65},{193,129... | collective-permute-start | bytes 786440 | tf_op jit(solution)/shard_map/ppermute | solution.py:21
  57.1 0.6 copy-start.10
  57.1 0.6 copy-start.12
  58.6 21.8 %collective-permute-start.16 = (bf16[384,1024]{1,0:T(8,128)(2,1)}, bf16[384,1024]{1,0:T(8,128)(2,1)S(1)}, u32[]{:S(2)}, u32[]{:S(2)}) collective-permute-start(bf16[384,1024]{1,0:T(8,128)(2,1)} %maximum_maximum_fusion), channel_id=1, source_target_pairs={{0,64},{64,128},{128,192},{192,1},{1,65},{65,129},{129,193},{193,0... | collective-permute-start | bytes 2359304 | tf_op jit(solution)/shard_map/ppermute | solution.py:21
  58.7 22.1 %collective-permute-start.15 = (bf16[384,1024]{1,0:T(8,128)(2,1)}, bf16[384,1024]{1,0:T(8,128)(2,1)}, u32[]{:S(2)}, u32[]{:S(2)}) collective-permute-start(bf16[384,1024]{1,0:T(8,128)(2,1)} %maximum_maximum_fusion), channel_id=1, source_target_pairs={{0,193},{64,0},{128,64},{192,128},{1,192},{65,1},{129,65},{193,129... | collective-permute-start | bytes 2359304 | tf_op jit(solution)/shard_map/ppermute | solution.py:21
  64.0 22.2 %collective-permute-start.4 = (bf16[32,4096]{1,0:T(8,128)(2,1)}, bf16[32,4096]{1,0:T(8,128)(2,1)}, u32[]{:S(2)}, u32[]{:S(2)}) collective-permute-start(bf16[32,4096]{1,0:T(8,128)(2,1)} %get-tuple-element.15), channel_id=1, source_target_pairs={{0,64},{64,128},{128,192},{192,1},{1,65},{65,129},{129,193},{193,0... | collective-permute-start | bytes 786440 | tf_op jit(solution)/shard_map/ppermute | solution.py:21
  64.0 22.2 %collective-permute-start.9 = (bf16[32,4096]{1,0:T(8,128)(2,1)}, bf16[32,4096]{1,0:T(8,128)(2,1)}, u32[]{:S(2)}, u32[]{:S(2)}) collective-permute-start(bf16[32,4096]{1,0:T(8,128)(2,1)} %get-tuple-element.16), channel_id=1, source_target_pairs={{0,193},{64,0},{128,64},{192,128},{1,192},{65,1},{129,65},{193,129... | collective-permute-start | bytes 786440 | tf_op jit(solution)/shard_map/ppermute | solution.py:21
  67.3 24.1 %copy-start.11 = (bf16[128,256]{1,0:T(8,128)(2,1)S(1)}, bf16[128,256]{1,0:T(8,128)(2,1)}, u32[]{:S(2)}) copy-start(bf16[128,256]{1,0:T(8,128)(2,1)} %copy-done.10) | copy-start | bytes 196612
  67.3 24.1 %copy-start.13 = (bf16[128,256]{1,0:T(8,128)(2,1)S(1)}, bf16[128,256]{1,0:T(8,128)(2,1)}, u32[]{:S(2)}) copy-start(bf16[128,256]{1,0:T(8,128)(2,1)} %copy-done.12) | copy-start | bytes 196612
  80.5 13.5 %collective-permute-start.17 = (bf16[192,1024]{1,0:T(8,128)(2,1)S(1)}, bf16[192,1024]{1,0:T(8,128)(2,1)S(1)}, u32[]{:S(2)}, u32[]{:S(2)}) collective-permute-start(bf16[192,1024]{1,0:T(8,128)(2,1)S(1)} %slice.158), channel_id=1, source_target_pairs={{0,64},{64,128},{128,192},{192,1},{1,65},{65,129},{129,193},{193,0... | collective-permute-start | bytes 1179656 | tf_op jit(solution)/shard_map/ppermute | solution.py:21
  81.8 12.2 %collective-permute-start.18 = (bf16[192,1024]{1,0:T(8,128)(2,1)S(1)}, bf16[192,1024]{1,0:T(8,128)(2,1)S(1)}, u32[]{:S(2)}, u32[]{:S(2)}) collective-permute-start(bf16[192,1024]{1,0:T(8,128)(2,1)S(1)} %slice.159), channel_id=1, source_target_pairs={{0,193},{64,0},{128,64},{192,128},{1,192},{65,1},{129,65},{193,129... | collective-permute-start | bytes 1179656 | tf_op jit(solution)/shard_map/ppermute | solution.py:21
  88.2 10.8 %copy-start.9 = (bf16[224,4096]{1,0:T(8,128)(2,1)S(1)}, bf16[224,4096]{1,0:T(8,128)(2,1)}, u32[]{:S(2)}) copy-start(bf16[224,4096]{1,0:T(8,128)(2,1)} %get-tuple-element.43) | copy-start | bytes 5505028
  88.2 8.4 %collective-permute-start.10 = (bf16[32,4096]{1,0:T(8,128)(2,1)S(1)}, bf16[32,4096]{1,0:T(8,128)(2,1)S(1)}, u32[]{:S(2)}, u32[]{:S(2)}) collective-permute-start(bf16[32,4096]{1,0:T(8,128)(2,1)S(1)} %get-tuple-element.14), channel_id=1, source_target_pairs={{0,193},{64,0},{128,64},{192,128},{1,192},{65,1},{129,65},{193,129... | collective-permute-start | bytes 786440 | tf_op jit(solution)/shard_map/ppermute | solution.py:21
  91.4 7.6 %collective-permute-start.5 = (bf16[32,4096]{1,0:T(8,128)(2,1)S(1)}, bf16[32,4096]{1,0:T(8,128)(2,1)S(1)}, u32[]{:S(2)}, u32[]{:S(2)}) collective-permute-start(bf16[32,4096]{1,0:T(8,128)(2,1)S(1)} %get-tuple-element.13), channel_id=1, source_target_pairs={{0,64},{64,128},{128,192},{192,1},{1,65},{65,129},{129,193},{193,0... | collective-permute-start | bytes 786440 | tf_op jit(solution)/shard_map/ppermute | solution.py:21
  99.8 6.4 %collective-permute-start.11 = (bf16[32,4096]{1,0:T(8,128)(2,1)S(1)}, bf16[32,4096]{1,0:T(8,128)(2,1)S(1)}, u32[]{:S(2)}, u32[]{:S(2)}) collective-permute-start(bf16[32,4096]{1,0:T(8,128)(2,1)S(1)} %get-tuple-element.12), channel_id=1, source_target_pairs={{0,193},{64,0},{128,64},{192,128},{1,192},{65,1},{129,65},{193,129... | collective-permute-start | bytes 786440 | tf_op jit(solution)/shard_map/ppermute | solution.py:21
  105.0 20.4 %collective-permute-start.19 = (bf16[4,384,1024]{2,1,0:T(8,128)(2,1)}, bf16[4,384,1024]{2,1,0:T(8,128)(2,1)}, u32[]{:S(2)}, u32[]{:S(2)}) collective-permute-start(bf16[4,384,1024]{2,1,0:T(8,128)(2,1)} %get-tuple-element.10), channel_id=1, source_target_pairs={{0,32},{32,0},{1,33},{33,1},{2,34},{34,2},{3,35},{35,3},{4,36},{36... | collective-permute-start | bytes 9437192 | tf_op jit(solution)/shard_map/ppermute | solution.py:25
  105.0 9.9 %collective-permute-start.6 = (bf16[32,4096]{1,0:T(8,128)(2,1)S(1)}, bf16[32,4096]{1,0:T(8,128)(2,1)S(1)}, u32[]{:S(2)}, u32[]{:S(2)}) collective-permute-start(bf16[32,4096]{1,0:T(8,128)(2,1)S(1)} %get-tuple-element.11), channel_id=1, source_target_pairs={{0,64},{64,128},{128,192},{192,1},{1,65},{65,129},{129,193},{193,0... | collective-permute-start | bytes 786440 | tf_op jit(solution)/shard_map/ppermute | solution.py:21
  106.3 9.3 %collective-permute-start.12 = (bf16[32,4096]{1,0:T(8,128)(2,1)S(1)}, bf16[32,4096]{1,0:T(8,128)(2,1)S(1)}, u32[]{:S(2)}, u32[]{:S(2)}) collective-permute-start(bf16[32,4096]{1,0:T(8,128)(2,1)S(1)} %get-tuple-element.59), channel_id=1, source_target_pairs={{0,193},{64,0},{128,64},{192,128},{1,192},{65,1},{129,65},{193,129... | collective-permute-start | bytes 786440 | tf_op jit(solution)/shard_map/ppermute | solution.py:21
  115.7 7.9 %collective-permute-start.13 = (bf16[32,4096]{1,0:T(8,128)(2,1)S(1)}, bf16[32,4096]{1,0:T(8,128)(2,1)S(1)}, u32[]{:S(2)}, u32[]{:S(2)}) collective-permute-start(bf16[32,4096]{1,0:T(8,128)(2,1)S(1)} %get-tuple-element.57), channel_id=1, source_target_pairs={{0,193},{64,0},{128,64},{192,128},{1,192},{65,1},{129,65},{193,129... | collective-permute-start | bytes 786440 | tf_op jit(solution)/shard_map/ppermute | solution.py:21
  125.3 13.2 %collective-permute-start.14 = (bf16[256,4096]{1,0:T(8,128)(2,1)}, bf16[256,4096]{1,0:T(8,128)(2,1)}, u32[]{:S(2)}, u32[]{:S(2)}) collective-permute-start(bf16[256,4096]{1,0:T(8,128)(2,1)} %pad_maximum_fusion.3.ra_ref), channel_id=1, source_target_pairs={{0,32},{32,0},{1,33},{33,1},{2,34},{34,2},{3,35},{35,3},{4,36},{36... | collective-permute-start | bytes 6291464 | tf_op jit(solution)/shard_map/ppermute | solution.py:25
  133.9 19.9 %copy-start.8 = (bf16[512,256]{1,0:T(8,128)(2,1)S(1)}, bf16[512,256]{1,0:T(8,128)(2,1)}, u32[]{:S(2)}) copy-start(bf16[512,256]{1,0:T(8,128)(2,1)} %down_proj.1) | copy-start | bytes 786436
  133.9 19.9 %collective-permute-start.20 = (bf16[512,256]{1,0:T(8,128)(2,1)}, bf16[512,256]{1,0:T(8,128)(2,1)S(1)}, u32[]{:S(2)}, u32[]{:S(2)}) collective-permute-start(bf16[512,256]{1,0:T(8,128)(2,1)} %down_proj.1), channel_id=1, source_target_pairs={{0,6},{2,0},{4,2},{6,4},{1,7},{3,1},{5,3},{7,5},{8,14},{10,8},{12,... | collective-permute-start | bytes 786440 | tf_op jit(solution)/shard_map/ppermute | solution.py:29
  137.1 16.7 %collective-permute-start.21 = (bf16[512,256]{1,0:T(8,128)(2,1)}, bf16[512,256]{1,0:T(8,128)(2,1)S(1)}, u32[]{:S(2)}, u32[]{:S(2)}) collective-permute-start(bf16[512,256]{1,0:T(8,128)(2,1)} %down_proj.1), channel_id=1, source_target_pairs={{0,4},{2,6},{4,0},{6,2},{1,5},{3,7},{5,1},{7,3},{8,12},{10,14},{12... | collective-permute-start | bytes 786440 | tf_op jit(solution)/shard_map/ppermute | solution.py:29
  137.5 16.3 %collective-permute-start.22 = (bf16[512,256]{1,0:T(8,128)(2,1)}, bf16[512,256]{1,0:T(8,128)(2,1)S(1)}, u32[]{:S(2)}, u32[]{:S(2)}) collective-permute-start(bf16[512,256]{1,0:T(8,128)(2,1)} %down_proj.1), channel_id=1, source_target_pairs={{0,2},{2,4},{4,6},{6,0},{1,3},{3,5},{5,7},{7,1},{8,10},{10,12},{12... | collective-permute-start | bytes 786440 | tf_op jit(solution)/shard_map/ppermute | solution.py:29
  154.0 1.2 copy-start.7
  157.1 23.4 %copy-start.16 = (s32[256]{0:T(256)S(1)}, s32[256]{0:T(256)}, u32[]{:S(2)}) copy-start(s32[256]{0:T(256)} %param.21) | copy-start | bytes 3076
  157.1 2.0 collective-permute-start.23
  174.4 16.1 %all-to-all-start.1 = ((bf16[16,16,1024]{2,1,0:T(8,128)(2,1)}), bf16[16,16,1024]{2,1,0:T(8,128)(2,1)S(1)}, u32[]{:S(2)}, u32[]{:S(2)}) async-start(bf16[16,16,1024]{2,1,0:T(8,128)(2,1)} %broadcast_in_dim.14), calls=%async_computation.1 | async-start | bytes 1048576 | tf_op jit(solution)/shard_map/all_to_all | solution.py:222
  196.3 17.2 %all-to-all-start.2 = ((f32[16,18,128]{2,1,0:T(8,128)}), f32[16,18,128]{2,1,0:T(8,128)S(1)}, u32[]{:S(2)}, u32[]{:S(2)}) async-start(f32[16,18,128]{2,1,0:T(8,128)} %broadcast_in_dim.15), calls=%async_computation.2 | async-start | bytes 393216 | tf_op jit(solution)/shard_map/all_to_all | solution.py:236
  213.6 18.9 %copy-start.1 = (bf16[1024,1024]{1,0:T(8,128)(2,1)S(1)}, bf16[1024,1024]{1,0:T(8,128)(2,1)}, u32[]{:S(2)}) copy-start(bf16[1024,1024]{1,0:T(8,128)(2,1)} %param.20) | copy-start | bytes 6291460
Sparse Core Ops, SparseCore 0:
  11.6 88.9 all-gather.2
